TPU v7x, 32 devices: a whole 2x2x4 slice. The times are simulated.
32 devices in a mesh: shard: 4 (over z), tensor: 2 (over core), section: 4 (over y, x).
Axes of the slice: x: 2, y: 2, z: 4, core: 2. Of those that a mesh axis runs over, the one named last changes fastest.
Arguments:
- gradient: bfloat16 [2560, 2560], P('shard', ('tensor', 'section')), may hold values from -100 to 100
- gain_grad: float32 [2, 2560], P(None, 'shard'), may hold values from -12 to 12
- left_statistic: float32 [2560, 2560], P('shard', ('tensor', 'section')), may hold values from -1 to 3, as said below
- left_basis: float32 [2560, 2560], P('shard', ('tensor', 'section')), may hold values from -1 to 1.5
- first_moment: float32 [2560, 2560], P('shard', ('tensor', 'section')), may hold values from -3 to 3
- second_moment: float32 [2560, 2560], P('shard', ('tensor', 'section')), may hold values from 0.2 to 2
- norm_gains: float32 [2, 2560], P(None, 'shard'), may hold values from 0.5 to 1.5
- gain_first: float32 [2, 2560], P(None, 'shard'), may hold values from -2 to 2
- gain_second: float32 [2, 2560], P(None, 'shard'), may hold values from 0.5 to 5
Outputs:
- update: float32 [2560, 2560], P('shard', ('tensor', 'section'))
- new_first: float32 [2560, 2560], P('shard', ('tensor', 'section'))
- new_second: float32 [2560, 2560], P('shard', ('tensor', 'section'))
- new_statistic: float32 [2560, 2560], P('shard', ('tensor', 'section'))
- new_basis: float32 [2560, 2560], P('shard', ('tensor', 'section'))
- new_gains: float32 [2, 2560], P(None, 'shard')
- new_gain_first: float32 [2, 2560], P(None, 'shard')
- new_gain_second: float32 [2, 2560], P(None, 'shard')
Inputs may be any that keep to these rules, and one draw needn't show every extreme that they name: `left_statistic`: symmetric.
All inputs are finite; a program needn't handle non-finite values.
Results may differ from a plain program's by a relative error of at most 0.0003.
Values may be sent and summed in bfloat16 or wider, within the bound.
A program may use at most 128 MiB of HBM per device.

v0:
```python
import jax
import jax.numpy as jnp
from jax import lax
from jax.sharding import PartitionSpec as P

D = 2560
NS_STEPS = 3


def matmul(left_side, right_side):
    return jnp.dot(
        left_side, right_side, precision=lax.Precision.HIGHEST, preferred_element_type=jnp.float32
    )


def times_rows(full_rows, segment):
    return matmul(full_rows, segment)


def transposed_terms(full_rows, local_block):
    return matmul(full_rows.T, local_block)


def row_panel(local_block):
    return lax.all_gather(local_block, ("tensor", "section"), axis=1, tiled=True)


def on_device(
    gradient,
    gain_grad,
    left_statistic,
    left_basis,
    first_moment,
    second_moment,
    norm_gains,
    gain_first,
    gain_second,
):
    group_size = lax.axis_size(("tensor", "section"))
    grad_float = gradient.astype(jnp.float32)
    local_sum = jnp.sum(grad_float * grad_float) + jnp.sum(gain_grad * gain_grad) / group_size
    squares_total = lax.psum(local_sum, ("shard", "tensor", "section"))
    clip_factor = jnp.minimum(1.0, D / jnp.sqrt(squares_total + 1e-06))
    clipped = clip_factor * grad_float
    rotate_scale = 1.0
    outer_scale = 1.0
    basis_rows = row_panel(left_basis)
    rotated = rotate_scale * lax.psum_scatter(
        transposed_terms(basis_rows, clipped), "shard", scatter_dimension=0, tiled=True
    )
    partner = clip_factor * lax.all_gather(gradient, "shard", axis=0, tiled=True).astype(
        jnp.float32
    )
    outer_rows = matmul(clipped, partner.T)
    outer_part = lax.psum_scatter(
        outer_rows, ("tensor", "section"), scatter_dimension=1, tiled=True
    )
    new_statistic = 0.95 * left_statistic + 0.05 / D * (outer_scale * outer_part)
    new_first = 0.9 * first_moment + 0.1 * rotated
    new_second = 0.95 * second_moment + 0.05 * rotated * rotated
    direction = new_first / (jnp.sqrt(new_second) + 1e-08)
    update = times_rows(basis_rows, lax.all_gather(direction, "shard", axis=0, tiled=True))
    statistic_rows = row_panel(new_statistic)
    power_product = times_rows(
        statistic_rows, lax.all_gather(left_basis, "shard", axis=0, tiled=True)
    )
    power_sum = lax.psum(jnp.sum(power_product * power_product), ("shard", "tensor", "section"))
    iterate = 0.9 * jnp.sqrt(D / (power_sum + 1e-06)) * power_product
    for sweep_index in range(NS_STEPS):
        iterate_rows = row_panel(iterate)
        gram_block = lax.psum_scatter(
            transposed_terms(iterate_rows, iterate), "shard", scatter_dimension=0, tiled=True
        )
        applied = times_rows(iterate_rows, lax.all_gather(gram_block, "shard", axis=0, tiled=True))
        iterate = 1.5 * iterate - 0.5 * applied
    gain_clipped = clip_factor * gain_grad
    new_gain_first = 0.9 * gain_first + 0.1 * gain_clipped
    new_gain_second = 0.95 * gain_second + 0.05 * gain_clipped * gain_clipped
    new_gains = norm_gains - 0.01 * new_gain_first / (jnp.sqrt(new_gain_second) + 1e-08)
    return (
        update,
        new_first,
        new_second,
        new_statistic,
        iterate,
        new_gains,
        new_gain_first,
        new_gain_second,
    )


def solution(mesh):
    return jax.shard_map(
        on_device,
        mesh=mesh,
        in_specs=(
            P("shard", ("tensor", "section")),
            P(None, "shard"),
            P("shard", ("tensor", "section")),
            P("shard", ("tensor", "section")),
            P("shard", ("tensor", "section")),
            P("shard", ("tensor", "section")),
            P(None, "shard"),
            P(None, "shard"),
            P(None, "shard"),
        ),
        out_specs=(
            P("shard", ("tensor", "section")),
            P("shard", ("tensor", "section")),
            P("shard", ("tensor", "section")),
            P("shard", ("tensor", "section")),
            P("shard", ("tensor", "section")),
            P(None, "shard"),
            P(None, "shard"),
            P(None, "shard"),
        ),
        check_vma=False,
    )
```

profile of v0, /device:TPU:0, one launch (start us, length us, event | category | flops | bytes accessed | tf_op | source)
XLA Modules:
  0.0 1141.1 jit_solution(16108901470709755)
XLA Ops:
  12.4 43.9 %psum.14 = f32[]{:T(128)} all-reduce(f32[]{:T(128)S(6)} %add.50), channel_id=1, replica_groups=mesh['shard'=4,'tensor'=2,'section'=4] {'shard','tensor','section'}, use_global_device_ids=true, to_apply=%region_2.0 | all-reduce | flops 1 | bytes 8 | tf_op jit(solution)/shard_map/psum | solution.py:42
  57.0 14.8 %fusion = f32[640,2560]{0,1:T(8,128)} fusion(bf16[2560,320]{0,1:T(8,128)(2,1)} %all-gather.16.cloned.1.call-done, f32[]{:T(128)S(6)} %min.3, bf16[640,320]{0,1:T(8,128)(2,1)} %param.9), kind=kOutput, calls=%fused_computation.1 | convolution fusion | flops 6293504000 | bytes 8601604 | tf_op jit(solution)/shard_map/dot_general | solution.py:11
  72.7 62.8 %reduce-scatter.8.cloned.1.call-done = f32[640,320]{0,1:T(8,128)} async-done(((f32[640,2560]{0,1:T(8,128)}), f32[640,320]{0,1:T(8,128)}) %reduce-scatter.8.cloned.1.call-update) | async-done | bytes 819216 | tf_op jit(solution)/shard_map/reduce_scatter | solution.py:55
  137.8 64.9 %all-gather.20.cloned.1.call-done = f32[2560,320]{0,1:T(8,128)} async-done(((f32[640,320]{0,1:T(8,128)}), f32[2560,320]{0,1:T(8,128)}) %all-gather.20.cloned.1.call-update) | async-done | bytes 3276816 | tf_op jit(solution)/shard_map/all_gather | solution.py:65
  202.7 47.8 %all-gather.18.cloned.1.call-done = f32[640,2560]{0,1:T(8,128)} async-done(((f32[640,320]{0,1:T(8,128)}), f32[640,2560]{0,1:T(8,128)}) %all-gather.18.cloned.1.call-update) | async-done | bytes 6553616 | tf_op jit(solution)/shard_map/all_gather | solution.py:25
  262.2 39.5 %psum.15 = f32[]{:T(128)} all-reduce(f32[]{:T(128)} %get-tuple-element.14), channel_id=1, replica_groups=mesh['shard'=4,'tensor'=2,'section'=4] {'shard','tensor','section'}, use_global_device_ids=true, to_apply=%region_6.0 | all-reduce | flops 1 | bytes 8 | tf_op jit(solution)/shard_map/psum | solution.py:67
  303.4 47.7 %all-gather.22.cloned.1.call-done = f32[640,2560]{0,1:T(8,128)} async-done(((f32[640,320]{0,1:T(8,128)}), f32[640,2560]{0,1:T(8,128)}) %all-gather.22.cloned.1.call-update) | async-done | bytes 6553616 | tf_op jit(solution)/shard_map/all_gather | solution.py:25
  351.1 15.1 %fusion.14 = f32[2560,320]{1,0:T(8,128)} fusion(f32[640,2560]{0,1:T(8,128)} %all-gather.22.cloned.1.call-done, f32[640,320]{0,1:T(8,128)} %broadcast_multiply_fusion), kind=kOutput, calls=%fused_computation.29 | convolution fusion | flops 6291456000 | bytes 10649600 | tf_op jit(solution)/shard_map/dot_general | solution.py:11
  366.3 72.8 %reduce-scatter.10.cloned.1.call-done = f32[640,320]{1,0:T(8,128)} async-done(((f32[2560,320]{1,0:T(8,128)}), f32[640,320]{1,0:T(8,128)}) %reduce-scatter.10.cloned.1.call-update) | async-done | bytes 819216 | tf_op jit(solution)/shard_map/reduce_scatter | solution.py:71
  439.4 78.2 %all-gather.24.cloned.1.call-done = f32[2560,320]{1,0:T(8,128)} async-done(((f32[640,320]{1,0:T(8,128)}), f32[2560,320]{1,0:T(8,128)}) %all-gather.24.cloned.1.call-update) | async-done | bytes 3276816 | tf_op jit(solution)/shard_map/all_gather | solution.py:74
  517.6 12.1 %fusion.4 = f32[640,320]{0,1:T(8,128)} fusion(f32[640,2560]{0,1:T(8,128)} %all-gather.22.cloned.1.call-done, f32[2560,320]{1,0:T(8,128)} %all-gather.24.cloned.1.call-done, f32[640,320]{0,1:T(8,128)S(1)} %copy-done.2), kind=kOutput, calls=%fused_computation.9 | convolution fusion | flops 6292070400 | bytes 11468800 | tf_op jit(solution)/shard_map/dot_general | solution.py:11
  529.7 45.3 %all-gather.26.cloned.1.call-done = f32[640,2560]{0,1:T(8,128)} async-done(((f32[640,320]{0,1:T(8,128)}), f32[640,2560]{0,1:T(8,128)}) %all-gather.26.cloned.1.call-update) | async-done | bytes 6553616 | tf_op jit(solution)/shard_map/all_gather | solution.py:25
  575.0 15.1 %fusion.15 = f32[2560,320]{1,0:T(8,128)} fusion(f32[640,2560]{0,1:T(8,128)} %all-gather.26.cloned.1.call-done, f32[640,320]{0,1:T(8,128)} %fusion.4), kind=kOutput, calls=%fused_computation.30 | convolution fusion | flops 6291456000 | bytes 10649600 | tf_op jit(solution)/shard_map/dot_general | solution.py:11
  590.2 72.8 %reduce-scatter.12.cloned.1.call-done = f32[640,320]{1,0:T(8,128)} async-done(((f32[2560,320]{1,0:T(8,128)}), f32[640,320]{1,0:T(8,128)}) %reduce-scatter.12.cloned.1.call-update) | async-done | bytes 819216 | tf_op jit(solution)/shard_map/reduce_scatter | solution.py:71
  664.2 77.1 %all-gather.28.cloned.1.call-done = f32[2560,320]{1,0:T(8,128)} async-done(((f32[640,320]{1,0:T(8,128)}), f32[2560,320]{1,0:T(8,128)}) %all-gather.28.cloned.1.call-update) | async-done | bytes 3276816 | tf_op jit(solution)/shard_map/all_gather | solution.py:74
  741.3 12.1 %fusion.5 = f32[640,320]{0,1:T(8,128)} fusion(f32[640,2560]{0,1:T(8,128)} %all-gather.26.cloned.1.call-done, f32[2560,320]{1,0:T(8,128)} %all-gather.28.cloned.1.call-done, f32[640,320]{0,1:T(8,128)S(1)} %copy-done.1), kind=kOutput, calls=%fused_computation.10 | convolution fusion | flops 6292070400 | bytes 11468800 | tf_op jit(solution)/shard_map/dot_general | solution.py:11
  753.5 35.1 %all-gather.12.cloned.1.call-done = f32[640,2560]{0,1:T(8,128)} async-done(((f32[640,320]{0,1:T(8,128)}), f32[640,2560]{0,1:T(8,128)}) %all-gather.12.cloned.1.call-update) | async-done | bytes 6553616 | tf_op jit(solution)/shard_map/all_gather | solution.py:25
  800.2 37.5 %all-gather.30.cloned.1.call-done = f32[640,2560]{0,1:T(8,128)} async-done(((f32[640,320]{0,1:T(8,128)}), f32[640,2560]{0,1:T(8,128)}) %all-gather.30.cloned.1.call-update) | async-done | bytes 6553616 | tf_op jit(solution)/shard_map/all_gather | solution.py:25
  837.7 14.8 %fusion.16 = f32[2560,320]{1,0:T(8,128)} fusion(f32[640,2560]{0,1:T(8,128)} %all-gather.30.cloned.1.call-done, f32[640,320]{0,1:T(8,128)S(1)} %copy-done), kind=kOutput, calls=%fused_computation.31 | convolution fusion | flops 6291456000 | bytes 10649600 | tf_op jit(solution)/shard_map/dot_general | solution.py:11
  852.7 49.8 %reduce-scatter.6.cloned.1.call-done = f32[640,320]{0,1:T(8,128)} async-done(((f32[2560,320]{0,1:T(8,128)}), f32[640,320]{0,1:T(8,128)}) %reduce-scatter.6.cloned.1.call-update) | async-done | bytes 819216 | tf_op jit(solution)/shard_map/reduce_scatter | solution.py:48
  905.5 72.0 %reduce-scatter.14.cloned.1.call-done = f32[640,320]{1,0:T(8,128)} async-done(((f32[2560,320]{1,0:T(8,128)}), f32[640,320]{1,0:T(8,128)}) %reduce-scatter.14.cloned.1.call-update) | async-done | bytes 819216 | tf_op jit(solution)/shard_map/reduce_scatter | solution.py:71
  978.3 67.4 %all-gather.14.cloned.1.call-done = f32[2560,320]{0,1:T(8,128)} async-done(((f32[640,320]{0,1:T(8,128)}), f32[2560,320]{0,1:T(8,128)}) %all-gather.14.cloned.1.call-update) | async-done | bytes 3276816 | tf_op jit(solution)/shard_map/all_gather | solution.py:62
  1057.4 64.9 %all-gather.32.cloned.1.call-done = f32[2560,320]{1,0:T(8,128)} async-done(((f32[640,320]{1,0:T(8,128)}), f32[2560,320]{1,0:T(8,128)}) %all-gather.32.cloned.1.call-update) | async-done | bytes 3276816 | tf_op jit(solution)/shard_map/all_gather | solution.py:74
  1122.3 12.1 %fusion.6 = f32[640,320]{0,1:T(8,128)} fusion(f32[640,2560]{0,1:T(8,128)} %all-gather.30.cloned.1.call-done, f32[2560,320]{1,0:T(8,128)} %all-gather.32.cloned.1.call-done, f32[640,320]{0,1:T(8,128)S(1)} %copy-done), kind=kOutput, calls=%fused_computation.11 | convolution fusion | flops 6292070400 | bytes 11468800 | tf_op jit(solution)/shard_map/dot_general | solution.py:11
  (64 shorter events, 48.5 us)
Async XLA Ops:
  7.2 49.9 %all-gather.16.cloned.1.call-start = ((), (), s32[]{:S(2)}) async-start(), calls=%async_computation.8 | async-start | bytes 2048000 | tf_op jit(solution)/shard_map/all_gather | solution.py:51
  7.9 127.5 %reduce-scatter.8.cloned.1.call-start = ((), (), s32[]{:S(2)}) async-start(), calls=%async_computation.9 | async-start | bytes 7372800 | tf_op jit(solution)/shard_map/reduce_scatter | solution.py:55
  71.9 130.8 %all-gather.20.cloned.1.call-start = ((), (), s32[]{:S(2)}) async-start(), calls=%async_computation.11 | async-start | bytes 4096000 | tf_op jit(solution)/shard_map/all_gather | solution.py:65
  72.6 177.9 %all-gather.18.cloned.1.call-start = ((), (), s32[]{:S(2)}) async-start(), calls=%async_computation.10 | async-start | bytes 7372800 | tf_op jit(solution)/shard_map/all_gather | solution.py:25
  137.6 213.5 %all-gather.22.cloned.1.call-start = ((), (), s32[]{:S(2)}) async-start(), calls=%async_computation.12 | async-start | bytes 7372800 | tf_op jit(solution)/shard_map/all_gather | solution.py:25
  303.4 135.7 %reduce-scatter.10.cloned.1.call-start = ((), (), s32[]{:S(2)}) async-start(), calls=%async_computation.13 | async-start | bytes 4915200 | tf_op jit(solution)/shard_map/reduce_scatter | solution.py:71
  366.2 151.4 %copy-start.2 = (f32[640,320]{0,1:T(8,128)S(1)}, f32[640,320]{0,1:T(8,128)}, u32[]{:S(2)}) copy-start(f32[640,320]{0,1:T(8,128)} %broadcast_multiply_fusion) | copy-start | bytes 2457604
  366.2 151.3 %all-gather.24.cloned.1.call-start = ((), (), s32[]{:S(2)}) async-start(), calls=%async_computation.14 | async-start | bytes 4915200 | tf_op jit(solution)/shard_map/all_gather | solution.py:74
  439.1 135.9 %all-gather.26.cloned.1.call-start = ((), (), s32[]{:S(2)}) async-start(), calls=%async_computation.15 | async-start | bytes 7372800 | tf_op jit(solution)/shard_map/all_gather | solution.py:25
  529.7 133.3 %reduce-scatter.12.cloned.1.call-start = ((), (), s32[]{:S(2)}) async-start(), calls=%async_computation.16 | async-start | bytes 4915200 | tf_op jit(solution)/shard_map/reduce_scatter | solution.py:71
  590.1 151.2 %copy-start.1 = (f32[640,320]{0,1:T(8,128)S(1)}, f32[640,320]{0,1:T(8,128)}, u32[]{:S(2)}) copy-start(f32[640,320]{0,1:T(8,128)} %fusion.4) | copy-start | bytes 2457604
  590.1 151.2 %all-gather.28.cloned.1.call-start = ((), (), s32[]{:S(2)}) async-start(), calls=%async_computation.17 | async-start | bytes 4915200 | tf_op jit(solution)/shard_map/all_gather | solution.py:74
  663.0 125.6 %all-gather.12.cloned.1.call-start = ((), (), s32[]{:S(2)}) async-start(), calls=%async_computation.5 | async-start | bytes 7372800 | tf_op jit(solution)/shard_map/all_gather | solution.py:25
  663.7 124.9 %copy-start.3 = (bf16[640,320]{0,1:T(8,128)(2,1)S(1)}, bf16[640,320]{0,1:T(8,128)(2,1)}, u32[]{:S(2)}) copy-start(bf16[640,320]{0,1:T(8,128)(2,1)} %param.9) | copy-start | bytes 1228804
  663.8 174.0 %all-gather.30.cloned.1.call-start = ((), (), s32[]{:S(2)}) async-start(), calls=%async_computation.18 | async-start | bytes 7372800 | tf_op jit(solution)/shard_map/all_gather | solution.py:25
  753.4 84.3 %copy-start = (f32[640,320]{0,1:T(8,128)S(1)}, f32[640,320]{0,1:T(8,128)}, u32[]{:S(2)}) copy-start(f32[640,320]{0,1:T(8,128)} %fusion.5) | copy-start | bytes 2457604
  753.4 149.0 %reduce-scatter.6.cloned.1.call-start = ((), (), s32[]{:S(2)}) async-start(), calls=%async_computation.6 | async-start | bytes 4096000 | tf_op jit(solution)/shard_map/reduce_scatter | solution.py:48
  800.0 177.6 %reduce-scatter.14.cloned.1.call-start = ((), (), s32[]{:S(2)}) async-start(), calls=%async_computation.19 | async-start | bytes 4915200 | tf_op jit(solution)/shard_map/reduce_scatter | solution.py:71
  852.6 125.0 %copy-start.7 = (f32[2,640]{1,0:T(2,128)S(1)}, f32[2,640]{1,0:T(2,128)}, u32[]{:S(2)}) copy-start(f32[2,640]{1,0:T(2,128)} %param.10) | copy-start | bytes 15364
  852.6 125.0 %copy-start.8 = (f32[2,640]{1,0:T(2,128)S(1)}, f32[2,640]{1,0:T(2,128)}, u32[]{:S(2)}) copy-start(f32[2,640]{1,0:T(2,128)} %param.15) | copy-start | bytes 15364
  852.6 125.0 %copy-start.9 = (f32[2,640]{1,0:T(2,128)S(1)}, f32[2,640]{1,0:T(2,128)}, u32[]{:S(2)}) copy-start(f32[2,640]{1,0:T(2,128)} %param.16) | copy-start | bytes 15364
  852.6 125.0 %copy-start.10 = (f32[2,640]{1,0:T(2,128)S(1)}, f32[2,640]{1,0:T(2,128)}, u32[]{:S(2)}) copy-start(f32[2,640]{1,0:T(2,128)} %param.17) | copy-start | bytes 15364
  852.6 193.0 %all-gather.14.cloned.1.call-start = ((), (), s32[]{:S(2)}) async-start(), calls=%async_computation.7 | async-start | bytes 4096000 | tf_op jit(solution)/shard_map/all_gather | solution.py:62
  905.3 217.0 %all-gather.32.cloned.1.call-start = ((), (), s32[]{:S(2)}) async-start(), calls=%async_computation.20 | async-start | bytes 4915200 | tf_op jit(solution)/shard_map/all_gather | solution.py:74
  (3 other events, 163.4 us)
Sparse Core Ops, SparseCore 0:
  9.6 41.7 all-gather.15
  72.0 63.3 reduce-scatter.7
  137.1 65.5 all-gather.19
  205.2 45.2 all-gather.17
  303.5 47.5 all-gather.21
  366.4 72.6 reduce-scatter.9
  440.7 76.7 all-gather.23
  529.8 45.1 all-gather.25
  590.3 72.6 reduce-scatter.11
  664.5 76.7 all-gather.27
  743.4 45.1 all-gather.11
  791.1 46.6 all-gather.29
  840.1 62.2 reduce-scatter.5
  904.7 72.7 reduce-scatter.13
  979.6 65.9 all-gather.13
  1047.2 75.0 all-gather.31
where the time goes:
time: 1150 us; the launch traced here: 1140 us
  waiting for transfers between devices  898 us (78%)
  matrix products  131 us (11%)
  blocking collectives  83.5 us (7%)
  between operations  17 us (1%)
    all_gather x3, waiting for transfers between devices, on_device(): lax.all_gather(gram_block, 'shard', axis=0, tiled=True)  220 us
    reduce_scatter x3, waiting for transfers between devices, on_device(): lax.psum_scatter(transposed_terms(iterate_rows, iterate), 'shard', scatte...  218 us
    all_gather x5, waiting for transfers between devices, row_panel(): lax.all_gather(local_block, ('tensor', 'section'), axis=1, tiled=True)  213 us
    dot_general x10, matrix products, matmul(): jnp.dot(left_side, right_side, precision=lax.Precision.HIGHEST, preferred...  131 us
    all_gather x1, waiting for transfers between devices, on_device(): lax.all_gather(direction, 'shard', axis=0, tiled=True)  67.4 us
    all_gather x1, waiting for transfers between devices, on_device(): lax.all_gather(left_basis, 'shard', axis=0, tiled=True)  64.9 us
    reduce_scatter x1, waiting for transfers between devices, on_device(): lax.psum_scatter(outer_rows, ('tensor', 'section'), scatter_dimension=1,...  62.8 us
    reduce_scatter x1, waiting for transfers between devices, on_device(): lax.psum_scatter(transposed_terms(basis_rows, clipped), 'shard', scatter_...  49.8 us
  transfers between devices with their start and end apart: 16, of which 15 were waited for; matrix products, arithmetic and copies ran while one was open for 5% of the time, Pallas kernels for 0%

commit v1 on v0

--- a/solution.py
+++ b/solution.py
@@ -5,6 +5,24 @@
 
 D = 2560
 NS_STEPS = 3
+
+
+def ring_gather(value, axis, dim):
+    ways, here, step = (lax.axis_size(axis), lax.axis_index(axis), value.shape[dim])
+    dims = [n * ways if d == dim else n for d, n in enumerate(value.shape)]
+    full = lax.dynamic_update_slice_in_dim(
+        jnp.zeros(dims, value.dtype), value, here * step, axis=dim
+    )
+    going_up = going_down = value
+    for far in range(1, ways // 2 + 1):
+        going_up = lax.ppermute(going_up, axis, [(d, (d + 1) % ways) for d in range(ways)])
+        full = lax.dynamic_update_slice_in_dim(full, going_up, (here - far) % ways * step, axis=dim)
+        if 2 * far < ways:
+            going_down = lax.ppermute(going_down, axis, [(d, (d - 1) % ways) for d in range(ways)])
+            full = lax.dynamic_update_slice_in_dim(
+                full, going_down, (here + far) % ways * step, axis=dim
+            )
+    return full
 
 
 def matmul(left_side, right_side):
@@ -61,9 +79,7 @@
     direction = new_first / (jnp.sqrt(new_second) + 1e-08)
     update = times_rows(basis_rows, lax.all_gather(direction, "shard", axis=0, tiled=True))
     statistic_rows = row_panel(new_statistic)
-    power_product = times_rows(
-        statistic_rows, lax.all_gather(left_basis, "shard", axis=0, tiled=True)
-    )
+    power_product = times_rows(statistic_rows, ring_gather(left_basis, "shard", 0))
     power_sum = lax.psum(jnp.sum(power_product * power_product), ("shard", "tensor", "section"))
     iterate = 0.9 * jnp.sqrt(D / (power_sum + 1e-06)) * power_product
     for sweep_index in range(NS_STEPS):

time: 1150 us -> 1090 us (0.948)
  waiting for transfers between devices: 898 us -> 834 us
    all_gather x1 -> x0, waiting for transfers between devices: 64.9 us -> none  [on_device(): lax.all_gather(left_basis, 'shard', axis=0, tiled=True)]
    all_gather x5, waiting for transfers between devices: 213 us -> 165 us  [row_panel(): lax.all_gather(local_block, ('tensor', 'section'), axis=1, tiled=True)]
    ppermute x0 -> x3, waiting for transfers between devices: none -> 48.5 us  [the longest x2 35.9 us: ring_gather(): lax.ppermute(going_up, axis, [(d, (d + 1) % ways) for d in range(ways)])]
  transfers between devices with their start and end apart: 16 -> 18, of which waited for: 15 -> 16; matrix products, arithmetic and copies ran while one was open for 5% -> 6% of each run, Pallas kernels for 0% -> 0%
where the time goes in v1:
time: 1090 us
  waiting for transfers between devices  834 us (77%)
  matrix products  131 us (12%)
  blocking collectives  81.7 us (7%)
  between operations  17.1 us (2%)
    all_gather x3, waiting for transfers between devices, on_device(): lax.all_gather(gram_block, 'shard', axis=0, tiled=True)  221 us
    reduce_scatter x3, waiting for transfers between devices, on_device(): lax.psum_scatter(transposed_terms(iterate_rows, iterate), 'shard', scatte...  218 us
    all_gather x5, waiting for transfers between devices, row_panel(): lax.all_gather(local_block, ('tensor', 'section'), axis=1, tiled=True)  165 us
    dot_general x10, matrix products, matmul(): jnp.dot(left_side, right_side, precision=lax.Precision.HIGHEST, preferred...  131 us
    all_gather x1, waiting for transfers between devices, on_device(): lax.all_gather(direction, 'shard', axis=0, tiled=True)  67.4 us
    reduce_scatter x1, waiting for transfers between devices, on_device(): lax.psum_scatter(outer_rows, ('tensor', 'section'), scatter_dimension=1,...  63.5 us
    reduce_scatter x1, waiting for transfers between devices, on_device(): lax.psum_scatter(transposed_terms(basis_rows, clipped), 'shard', scatter_...  49.6 us
    psum x1, blocking collectives, on_device(): squares_total = lax.psum(local_sum, ('shard', 'tensor', 'section'))  43.9 us
  transfers between devices with their start and end apart: 18, of which 16 were waited for; matrix products, arithmetic and copies ran while one was open for 6% of the time, Pallas kernels for 0%

profile of v1, /device:TPU:0, one launch (start us, length us, event | category | flops | bytes accessed | tf_op | source)
XLA Modules:
  0.0 1086.6 jit_solution(8951941868853338600)
XLA Ops:
  12.4 43.9 %psum.14 = f32[]{:T(128)} all-reduce(f32[]{:T(128)S(6)} %add.77), channel_id=1, replica_groups=mesh['shard'=4,'tensor'=2,'section'=4] {'shard','tensor','section'}, use_global_device_ids=true, to_apply=%region_2.0 | all-reduce | flops 1 | bytes 8 | tf_op jit(solution)/shard_map/psum | solution.py:60
  57.0 14.8 %fusion = f32[640,2560]{0,1:T(8,128)} fusion(bf16[2560,320]{0,1:T(8,128)(2,1)} %all-gather.15.cloned.1.call-done, f32[]{:T(128)S(6)} %min.3, bf16[640,320]{0,1:T(8,128)(2,1)} %param.9), kind=kOutput, calls=%fused_computation.1 | convolution fusion | flops 6293504000 | bytes 8601604 | tf_op jit(solution)/shard_map/dot_general | solution.py:29
  71.9 63.5 %reduce-scatter.8.cloned.1.call-done = f32[640,320]{0,1:T(8,128)} async-done(((f32[640,2560]{0,1:T(8,128)}), f32[640,320]{0,1:T(8,128)}) %reduce-scatter.8.cloned.1.call-update) | async-done | bytes 819216 | tf_op jit(solution)/shard_map/reduce_scatter | solution.py:73
  141.6 19.5 %collective-permute-done = f32[640,320]{0,1:T(8,128)} collective-permute-done((f32[640,320]{0,1:T(8,128)}, f32[640,320]{0,1:T(8,128)}, u32[]{:S(2)}, u32[]{:S(2)}) %collective-permute-start) | collective-permute-done | bytes 819232 | tf_op jit(solution)/shard_map/ppermute | solution.py:18
  164.7 12.6 %collective-permute-done.1 = f32[640,320]{0,1:T(8,128)} collective-permute-done((f32[640,320]{0,1:T(8,128)}, f32[640,320]{0,1:T(8,128)}, u32[]{:S(2)}, u32[]{:S(2)}) %collective-permute-start.1) | collective-permute-done | bytes 819232 | tf_op jit(solution)/shard_map/ppermute | solution.py:21
  178.6 16.4 %collective-permute-done.2 = f32[640,320]{0,1:T(8,128)} collective-permute-done((f32[640,320]{0,1:T(8,128)}, f32[640,320]{0,1:T(8,128)}, u32[]{:S(2)}, u32[]{:S(2)}) %collective-permute-start.2) | collective-permute-done | bytes 819232 | tf_op jit(solution)/shard_map/ppermute | solution.py:18
  196.3 12.1 %multiply_reduce_fusion = (f32[]{:T(128)}, f32[640,320]{0,1:T(8,128)}) fusion(f32[640,2560]{0,1:T(8,128)} %all-gather.17.cloned.1.call-done, f32[2560,320]{0,1:T(8,128)S(1)} %constant_dynamic-update-slice_fusion), kind=kOutput, calls=%fused_computation.17 | convolution fusion | flops 6291865600 | bytes 10649604 | tf_op jit(solution)/shard_map/dot_general | solution.py:29
  208.4 37.7 %psum.15 = f32[]{:T(128)} all-reduce(f32[]{:T(128)} %get-tuple-element.14), channel_id=1, replica_groups=mesh['shard'=4,'tensor'=2,'section'=4] {'shard','tensor','section'}, use_global_device_ids=true, to_apply=%region_6.7 | all-reduce | flops 1 | bytes 8 | tf_op jit(solution)/shard_map/psum | solution.py:83
  249.2 47.4 %all-gather.19.cloned.1.call-done = f32[640,2560]{0,1:T(8,128)} async-done(((f32[640,320]{0,1:T(8,128)}), f32[640,2560]{0,1:T(8,128)}) %all-gather.19.cloned.1.call-update) | async-done | bytes 6553616 | tf_op jit(solution)/shard_map/all_gather | solution.py:43
  296.6 15.1 %fusion.13 = f32[2560,320]{1,0:T(8,128)} fusion(f32[640,2560]{0,1:T(8,128)} %all-gather.19.cloned.1.call-done, f32[640,320]{0,1:T(8,128)} %broadcast_multiply_fusion), kind=kOutput, calls=%fused_computation.33 | convolution fusion | flops 6291456000 | bytes 10649600 | tf_op jit(solution)/shard_map/dot_general | solution.py:29
  311.8 72.8 %reduce-scatter.10.cloned.1.call-done = f32[640,320]{1,0:T(8,128)} async-done(((f32[2560,320]{1,0:T(8,128)}), f32[640,320]{1,0:T(8,128)}) %reduce-scatter.10.cloned.1.call-update) | async-done | bytes 819216 | tf_op jit(solution)/shard_map/reduce_scatter | solution.py:87
  384.6 78.3 %all-gather.21.cloned.1.call-done = f32[2560,320]{1,0:T(8,128)} async-done(((f32[640,320]{1,0:T(8,128)}), f32[2560,320]{1,0:T(8,128)}) %all-gather.21.cloned.1.call-update) | async-done | bytes 3276816 | tf_op jit(solution)/shard_map/all_gather | solution.py:90
  462.9 12.1 %multiply_subtract_fusion = f32[640,320]{0,1:T(8,128)} fusion(f32[640,320]{0,1:T(8,128)S(1)} %copy-done.2, f32[640,2560]{0,1:T(8,128)} %all-gather.19.cloned.1.call-done, f32[2560,320]{1,0:T(8,128)} %all-gather.21.cloned.1.call-done), kind=kOutput, calls=%fused_computation.16 | convolution fusion | flops 6292070400 | bytes 11468800 | tf_op jit(solution)/shard_map/dot_general | solution.py:29
  475.3 45.1 %all-gather.23.cloned.1.call-done = f32[640,2560]{0,1:T(8,128)} async-done(((f32[640,320]{0,1:T(8,128)}), f32[640,2560]{0,1:T(8,128)}) %all-gather.23.cloned.1.call-update) | async-done | bytes 6553616 | tf_op jit(solution)/shard_map/all_gather | solution.py:43
  520.4 15.1 %fusion.14 = f32[2560,320]{1,0:T(8,128)} fusion(f32[640,2560]{0,1:T(8,128)} %all-gather.23.cloned.1.call-done, f32[640,320]{0,1:T(8,128)} %multiply_subtract_fusion), kind=kOutput, calls=%fused_computation.34 | convolution fusion | flops 6291456000 | bytes 10649600 | tf_op jit(solution)/shard_map/dot_general | solution.py:29
  535.5 72.8 %reduce-scatter.12.cloned.1.call-done = f32[640,320]{1,0:T(8,128)} async-done(((f32[2560,320]{1,0:T(8,128)}), f32[640,320]{1,0:T(8,128)}) %reduce-scatter.12.cloned.1.call-update) | async-done | bytes 819216 | tf_op jit(solution)/shard_map/reduce_scatter | solution.py:87
  609.0 77.8 %all-gather.25.cloned.1.call-done = f32[2560,320]{1,0:T(8,128)} async-done(((f32[640,320]{1,0:T(8,128)}), f32[2560,320]{1,0:T(8,128)}) %all-gather.25.cloned.1.call-update) | async-done | bytes 3276816 | tf_op jit(solution)/shard_map/all_gather | solution.py:90
  699.4 34.5 %all-gather.11.cloned.1.call-done = f32[640,2560]{0,1:T(8,128)} async-done(((f32[640,320]{0,1:T(8,128)}), f32[640,2560]{0,1:T(8,128)}) %all-gather.11.cloned.1.call-update) | async-done | bytes 6553616 | tf_op jit(solution)/shard_map/all_gather | solution.py:43
  745.4 37.8 %all-gather.27.cloned.1.call-done = f32[640,2560]{0,1:T(8,128)} async-done(((f32[640,320]{0,1:T(8,128)}), f32[640,2560]{0,1:T(8,128)}) %all-gather.27.cloned.1.call-update) | async-done | bytes 6553616 | tf_op jit(solution)/shard_map/all_gather | solution.py:43
  783.2 14.8 %fusion.15 = f32[2560,320]{1,0:T(8,128)} fusion(f32[640,2560]{0,1:T(8,128)} %all-gather.27.cloned.1.call-done, f32[640,320]{0,1:T(8,128)S(1)} %copy-done), kind=kOutput, calls=%fused_computation.35 | convolution fusion | flops 6291456000 | bytes 10649600 | tf_op jit(solution)/shard_map/dot_general | solution.py:29
  798.2 49.6 %reduce-scatter.6.cloned.1.call-done = f32[640,320]{0,1:T(8,128)} async-done(((f32[2560,320]{0,1:T(8,128)}), f32[640,320]{0,1:T(8,128)}) %reduce-scatter.6.cloned.1.call-update) | async-done | bytes 819216 | tf_op jit(solution)/shard_map/reduce_scatter | solution.py:66
  850.9 72.2 %reduce-scatter.14.cloned.1.call-done = f32[640,320]{1,0:T(8,128)} async-done(((f32[2560,320]{1,0:T(8,128)}), f32[640,320]{1,0:T(8,128)}) %reduce-scatter.14.cloned.1.call-update) | async-done | bytes 819216 | tf_op jit(solution)/shard_map/reduce_scatter | solution.py:87
  923.8 67.4 %all-gather.13.cloned.1.call-done = f32[2560,320]{0,1:T(8,128)} async-done(((f32[640,320]{0,1:T(8,128)}), f32[2560,320]{0,1:T(8,128)}) %all-gather.13.cloned.1.call-update) | async-done | bytes 3276816 | tf_op jit(solution)/shard_map/all_gather | solution.py:80
  1002.9 64.9 %all-gather.29.cloned.1.call-done = f32[2560,320]{1,0:T(8,128)} async-done(((f32[640,320]{1,0:T(8,128)}), f32[2560,320]{1,0:T(8,128)}) %all-gather.29.cloned.1.call-update) | async-done | bytes 3276816 | tf_op jit(solution)/shard_map/all_gather | solution.py:90
  (72 shorter events, 71.1 us)
Async XLA Ops:
  7.2 49.9 %all-gather.15.cloned.1.call-start = ((), (), s32[]{:S(2)}) async-start(), calls=%async_computation.8 | async-start | bytes 2048000 | tf_op jit(solution)/shard_map/all_gather | solution.py:69
  7.9 127.6 %reduce-scatter.8.cloned.1.call-start = ((), (), s32[]{:S(2)}) async-start(), calls=%async_computation.9 | async-start | bytes 7372800 | tf_op jit(solution)/shard_map/reduce_scatter | solution.py:73
  71.9 124.4 %all-gather.17.cloned.1.call-start = ((), (), s32[]{:S(2)}) async-start(), calls=%async_computation.10 | async-start | bytes 7372800 | tf_op jit(solution)/shard_map/all_gather | solution.py:43
  137.6 159.0 %all-gather.19.cloned.1.call-start = ((), (), s32[]{:S(2)}) async-start(), calls=%async_computation.11 | async-start | bytes 7372800 | tf_op jit(solution)/shard_map/all_gather | solution.py:43
  137.7 23.3 %collective-permute-start = (f32[640,320]{0,1:T(8,128)}, f32[640,320]{0,1:T(8,128)}, u32[]{:S(2)}, u32[]{:S(2)}) collective-permute-start(f32[640,320]{0,1:T(8,128)} %param.12), channel_id=1, source_target_pairs={{0,8},{8,16},{16,24},{24,0},{1,9},{9,17},{17,25},{25,1},{2,10},{10... | collective-permute-start | bytes 2457608 | tf_op jit(solution)/shard_map/ppermute | solution.py:18
  139.2 38.1 %collective-permute-start.1 = (f32[640,320]{0,1:T(8,128)}, f32[640,320]{0,1:T(8,128)}, u32[]{:S(2)}, u32[]{:S(2)}) collective-permute-start(f32[640,320]{0,1:T(8,128)} %param.12), channel_id=1, source_target_pairs={{0,24},{8,0},{16,8},{24,16},{1,25},{9,1},{17,9},{25,17},{2,26},{10... | collective-permute-start | bytes 2457608 | tf_op jit(solution)/shard_map/ppermute | solution.py:21
  161.0 34.0 %collective-permute-start.2 = (f32[640,320]{0,1:T(8,128)}, f32[640,320]{0,1:T(8,128)}, u32[]{:S(2)}, u32[]{:S(2)}) collective-permute-start(f32[640,320]{0,1:T(8,128)} %collective-permute-done), channel_id=1, source_target_pairs={{0,8},{8,16},{16,24},{24,0},{1,9},{9,17},{17,25},{25,1},{2,10},{10... | collective-permute-start | bytes 2457608 | tf_op jit(solution)/shard_map/ppermute | solution.py:18
  249.0 135.6 %reduce-scatter.10.cloned.1.call-start = ((), (), s32[]{:S(2)}) async-start(), calls=%async_computation.12 | async-start | bytes 4915200 | tf_op jit(solution)/shard_map/reduce_scatter | solution.py:87
  311.7 151.2 %copy-start.2 = (f32[640,320]{0,1:T(8,128)S(1)}, f32[640,320]{0,1:T(8,128)}, u32[]{:S(2)}) copy-start(f32[640,320]{0,1:T(8,128)} %broadcast_multiply_fusion) | copy-start | bytes 2457604
  311.7 151.2 %all-gather.21.cloned.1.call-start = ((), (), s32[]{:S(2)}) async-start(), calls=%async_computation.13 | async-start | bytes 4915200 | tf_op jit(solution)/shard_map/all_gather | solution.py:90
  384.6 135.8 %all-gather.23.cloned.1.call-start = ((), (), s32[]{:S(2)}) async-start(), calls=%async_computation.14 | async-start | bytes 7372800 | tf_op jit(solution)/shard_map/all_gather | solution.py:43
  475.0 133.3 %reduce-scatter.12.cloned.1.call-start = ((), (), s32[]{:S(2)}) async-start(), calls=%async_computation.15 | async-start | bytes 4915200 | tf_op jit(solution)/shard_map/reduce_scatter | solution.py:87
  535.5 151.4 %copy-start.1 = (f32[640,320]{0,1:T(8,128)S(1)}, f32[640,320]{0,1:T(8,128)}, u32[]{:S(2)}) copy-start(f32[640,320]{0,1:T(8,128)} %multiply_subtract_fusion) | copy-start | bytes 2457604
  535.5 151.3 %all-gather.25.cloned.1.call-start = ((), (), s32[]{:S(2)}) async-start(), calls=%async_computation.16 | async-start | bytes 4915200 | tf_op jit(solution)/shard_map/all_gather | solution.py:90
  608.3 125.6 %all-gather.11.cloned.1.call-start = ((), (), s32[]{:S(2)}) async-start(), calls=%async_computation.5 | async-start | bytes 7372800 | tf_op jit(solution)/shard_map/all_gather | solution.py:43
  608.9 174.3 %all-gather.27.cloned.1.call-start = ((), (), s32[]{:S(2)}) async-start(), calls=%async_computation.17 | async-start | bytes 7372800 | tf_op jit(solution)/shard_map/all_gather | solution.py:43
  698.9 148.9 %reduce-scatter.6.cloned.1.call-start = ((), (), s32[]{:S(2)}) async-start(), calls=%async_computation.6 | async-start | bytes 4096000 | tf_op jit(solution)/shard_map/reduce_scatter | solution.py:66
  745.3 177.7 %reduce-scatter.14.cloned.1.call-start = ((), (), s32[]{:S(2)}) async-start(), calls=%async_computation.18 | async-start | bytes 4915200 | tf_op jit(solution)/shard_map/reduce_scatter | solution.py:87
  798.1 125.0 %copy-start.7 = (f32[2,640]{1,0:T(2,128)S(1)}, f32[2,640]{1,0:T(2,128)}, u32[]{:S(2)}) copy-start(f32[2,640]{1,0:T(2,128)} %param.10) | copy-start | bytes 15364
  798.1 125.0 %copy-start.8 = (f32[2,640]{1,0:T(2,128)S(1)}, f32[2,640]{1,0:T(2,128)}, u32[]{:S(2)}) copy-start(f32[2,640]{1,0:T(2,128)} %param.15) | copy-start | bytes 15364
  798.1 125.0 %copy-start.9 = (f32[2,640]{1,0:T(2,128)S(1)}, f32[2,640]{1,0:T(2,128)}, u32[]{:S(2)}) copy-start(f32[2,640]{1,0:T(2,128)} %param.16) | copy-start | bytes 15364
  798.1 125.0 %copy-start.10 = (f32[2,640]{1,0:T(2,128)S(1)}, f32[2,640]{1,0:T(2,128)}, u32[]{:S(2)}) copy-start(f32[2,640]{1,0:T(2,128)} %param.17) | copy-start | bytes 15364
  798.1 193.0 %all-gather.13.cloned.1.call-start = ((), (), s32[]{:S(2)}) async-start(), calls=%async_computation.7 | async-start | bytes 4096000 | tf_op jit(solution)/shard_map/all_gather | solution.py:80
  850.6 217.2 %all-gather.29.cloned.1.call-start = ((), (), s32[]{:S(2)}) async-start(), calls=%async_computation.19 | async-start | bytes 4915200 | tf_op jit(solution)/shard_map/all_gather | solution.py:90
  (5 other events, 372.4 us)
Sparse Core Ops, SparseCore 0:
  9.6 41.7 all-gather.14
  72.0 63.4 reduce-scatter.7
  138.1 46.6 all-gather.16
  249.1 47.4 all-gather.18
  311.9 72.6 reduce-scatter.9
  386.1 76.7 all-gather.20
  475.1 45.1 all-gather.22
  535.6 72.6 reduce-scatter.11
  610.0 76.7 all-gather.24
  688.7 45.1 all-gather.10
  736.6 46.6 all-gather.26
  785.5 62.2 reduce-scatter.5
  850.2 72.8 reduce-scatter.13
  925.2 65.9 all-gather.12
  992.7 75.0 all-gather.28
